TPU v7x, 32 devices: a whole 2x2x4 slice. The times are simulated.
32 devices in a mesh: region: 8 (over y, x, core), group: 4 (over z).
Axes of the slice: x: 2, y: 2, z: 4, core: 2. Of those that a mesh axis runs over, the one named last changes fastest.
Arguments:
- ensemble: bfloat16 [8192, 512], P(('region', 'group')), may hold values from -6 to 6
- tiles: bfloat16 [2, 256, 8192], P(None, None, ('region', 'group')), may hold values from -0.09375 to 0.09375
- tile_live: int32 [2, 8], replicated, may hold values 0 or 1
- observed: float32 [2, 256], replicated, may hold values from -6 to 6
- perturb: bfloat16 [2, 256, 512], replicated, may hold values from -6 to 6
- obs_var: float32 [2, 256], replicated, may hold values from 0.5 to 4
Outputs:
- analysis: bfloat16 [8192, 512], P(('region', 'group'))
All inputs are finite; a program needn't handle non-finite values. Where the computation divides by a largest or mean magnitude, that divisor is 1e-20 or more.
Results may differ from a plain program's by a relative error of at most 0.013.
Values may be sent and summed in bfloat16 or wider, within the bound.
A program may use at most 64 MiB of HBM per device.

v0:
```python
import functools

import jax
import jax.numpy as jnp
from jax import lax
from jax.experimental import pallas as pl
from jax.experimental.pallas import tpu as pltpu
from jax.sharding import PartitionSpec as P

NEWTON = 4
CORES = 2
PIECES = 2
F32 = jnp.float32
BF16 = jnp.bfloat16


def split(x):
    hi = x.astype(BF16)
    return hi, (x - hi.astype(F32)).astype(BF16)


def dot3(a, b):
    left = jnp.concatenate([a[0], a[0], a[1]], axis=1)
    right = jnp.concatenate([b[0], b[1], b[0]], axis=0)
    return jnp.dot(left, right, preferred_element_type=F32)


def dot_nt(a, b):
    return lax.dot_general(a, b, (((1,), (1,)), ((), ())), preferred_element_type=F32)


def kernel(
    region_count, group_count,
    ens_hbm, tiles_hbm, live_ref, obs_ref, pert_hbm, var_ref,
    out_ref,
    ens, tiles, pert, partial, rs_buf, z_send, z_buf, spread_buf,
    mean_part, mean_rs, mean_zsend, mean_z,
    pair_buf, half_buf,
    load_sem, rs_ssem, rs_rsem, z_ssem, z_rsem, ag_ssem, ag_rsem,
    mrs_ssem, mrs_rsem, mz_ssem, mz_rsem, pair_ssem, pair_rsem,
):
    batches, obs_count, members = pert.shape
    region = lax.axis_index("region")
    group = lax.axis_index("group")
    chunk_rows, chunk_cols = rs_buf.shape[2:]
    across = members // chunk_cols

    barrier = pltpu.get_barrier_semaphore()
    for k in range(1, region_count):
        pl.semaphore_signal(barrier, inc=1, device_id=(lax.rem(region + k, region_count), group), device_id_type=pl.DeviceIdType.MESH)
    for k in range(1, group_count):
        pl.semaphore_signal(barrier, inc=1, device_id=(region, lax.rem(group + k, group_count)), device_id_type=pl.DeviceIdType.MESH)

    loads = [pltpu.make_async_copy(ens_hbm, ens, load_sem.at[0])]
    loads += [pltpu.make_async_copy(tiles_hbm.at[b], tiles.at[b], load_sem.at[1 + b]) for b in range(batches)]
    loads += [pltpu.make_async_copy(pert_hbm.at[b], pert.at[b], load_sem.at[1 + batches + b]) for b in range(batches)]
    for load in loads[:1 + batches]:
        load.start()

    row_at = lax.broadcasted_iota(jnp.int32, (obs_count, obs_count), 0)
    col_at = lax.broadcasted_iota(jnp.int32, (obs_count, obs_count), 1)
    on_diag = row_at == col_at
    ident = jnp.where(on_diag, 1.0, 0.0).astype(F32)

    def as_row(column):
        return jnp.sum(jnp.where(on_diag, column, 0.0), axis=0, keepdims=True)

    def as_column(row):
        return jnp.sum(jnp.where(on_diag, row, 0.0), axis=1, keepdims=True)

    piece_cols = chunk_cols // PIECES

    def chunk(ref, index, piece=None):
        rows = pl.ds(pl.multiple_of(lax.div(index, across) * chunk_rows, chunk_rows), chunk_rows)
        start, width = (0, chunk_cols) if piece is None else (piece * piece_cols, piece_cols)
        if across > 1:
            start = pl.multiple_of(lax.rem(index, across) * chunk_cols + start, piece_cols)
        return ref.at[rows, pl.ds(start, width)]

    def part(ref, piece):
        return ref if piece is None else ref.at[:, pl.ds(piece * piece_cols, piece_cols)]

    def sem_row(b, piece):
        return b * PIECES + (piece or 0)

    def pieces_of(b):
        return range(PIECES) if b == 0 else (None,)

    def remote(src, dst, ssem, rsem, where):
        return pltpu.make_async_remote_copy(
            src_ref=src, dst_ref=dst, send_sem=ssem, recv_sem=rsem,
            device_id=where, device_id_type=pl.DeviceIdType.MESH,
        )

    region_peers = [lax.rem(region + k, region_count) for k in range(1, region_count)]
    group_peers = [lax.rem(group + k, group_count) for k in range(1, group_count)]
    sends = []

    def launch(copy):
        copy.start()
        sends.append(copy)

    def local_partial(b):
        loads[1 + b].wait()
        value = jnp.dot(tiles[b], ens[...], preferred_element_type=F32)
        value = value * live_ref[b, region].astype(F32)
        mean = jnp.mean(value, axis=1, keepdims=True)
        partial[b] = (value - mean).astype(BF16)
        return mean

    chips = region_count // CORES
    chip, core = lax.div(region, CORES), lax.rem(region, CORES)
    chip_order = [lax.rem(chip + 1 + k, chips) for k in range(chips)]
    chip_peers = chip_order[:-1]
    partner = chip * CORES + (CORES - 1 - core)

    def scatter(b, piece):
        row = sem_row(b, piece)
        for k, peer in enumerate(region_peers):
            launch(remote(chunk(partial.at[b], peer, piece), part(rs_buf.at[b, region], piece), rs_ssem.at[row, k], rs_rsem.at[row, region], (peer, group)))

    def scatter_pair(b):
        for k, there in enumerate(chip_order):
            launch(remote(chunk(partial.at[b], there * CORES + CORES - 1 - core), pair_buf.at[b, there], pair_ssem.at[b, k], pair_rsem.at[b, there], (partner, group)))

    def pair_sum(b, there):
        remote(pair_buf.at[b, there], pair_buf.at[b, there], pair_ssem.at[b, 0], pair_rsem.at[b, there], (partner, group)).wait_recv()
        return chunk(partial.at[b], there * CORES + core)[...].astype(F32) + pair_buf[b, there].astype(F32)

    def scatter_chips(b):
        row = sem_row(b, None)
        for k, there in enumerate(chip_peers):
            half_buf[b, there] = pair_sum(b, there).astype(BF16)
            launch(remote(half_buf.at[b, there], rs_buf.at[b, region], rs_ssem.at[row, k], rs_rsem.at[row, region], (there * CORES + core, group)))

    def sum_region(b, piece):
        row = sem_row(b, piece)
        if b == 0:
            total, peers = chunk(partial.at[b], region, piece)[...].astype(F32), region_peers
        else:
            total, peers = pair_sum(b, chip), [there * CORES + core for there in chip_peers]
        for peer in peers:
            block = part(rs_buf.at[b, peer], piece)
            remote(block, block, rs_ssem.at[row, 0], rs_rsem.at[row, peer], (peer, group)).wait_recv()
            total = total + block[...].astype(F32)
        mine = part(z_send.at[b], piece)
        mine[...] = total.astype(BF16)
        for k, peer in enumerate(group_peers):
            launch(remote(mine, part(z_buf.at[b, group], piece), z_ssem.at[row, k], z_rsem.at[row, group], (region, peer)))

    def sum_group(b, piece):
        row = sem_row(b, piece)
        total = part(z_send.at[b], piece)[...].astype(F32)
        for peer in group_peers:
            block = part(z_buf.at[b, peer], piece)
            remote(block, block, z_ssem.at[row, 0], z_rsem.at[row, peer], (region, peer)).wait_recv()
            total = total + block[...].astype(F32)
        mine = chunk(spread_buf.at[b], region, piece)
        mine[...] = total.astype(BF16)
        for k, peer in enumerate(region_peers):
            launch(remote(mine, mine, ag_ssem.at[row, k], ag_rsem.at[row, region], (peer, group)))

    def gathered(b):
        for piece in pieces_of(b):
            for peer in region_peers:
                block = chunk(spread_buf.at[b], peer, piece)
                row = sem_row(b, piece)
                remote(block, block, ag_ssem.at[row, 0], ag_rsem.at[row, peer], (peer, group)).wait_recv()
        return spread_buf[b]

    loads[0].wait()
    means = [local_partial(0)]
    pl.semaphore_wait(barrier, region_count - 1 + group_count - 1)
    for piece in pieces_of(0):
        scatter(0, piece)
    for load in loads[1 + batches:]:
        load.start()
    for b in range(1, batches):
        means.append(local_partial(b))
    for b in range(1, batches):
        scatter_pair(b)
    for b in range(batches):
        mean_part[:, b * obs_count:(b + 1) * obs_count] = as_row(means[b])
    for k, peer in enumerate(region_peers):
        launch(remote(mean_part, mean_rs.at[region], mrs_ssem.at[k], mrs_rsem.at[region], (peer, group)))
    for b in range(1, batches):
        scatter_chips(b)
    for piece in pieces_of(0):
        sum_region(0, piece)
    total = mean_part[...]
    for peer in region_peers:
        remote(mean_rs.at[peer], mean_rs.at[peer], mrs_ssem.at[0], mrs_rsem.at[peer], (peer, group)).wait_recv()
        total = total + mean_rs[peer]
    mean_zsend[...] = total
    for k, peer in enumerate(group_peers):
        launch(remote(mean_zsend, mean_z.at[group], mz_ssem.at[k], mz_rsem.at[group], (region, peer)))
    for b in range(1, batches):
        sum_region(b, None)
    for piece in pieces_of(0):
        sum_group(0, piece)
    mean_row = mean_zsend[...]
    for peer in group_peers:
        remote(mean_z.at[peer], mean_z.at[peer], mz_ssem.at[0], mz_rsem.at[peer], (region, peer)).wait_recv()
        mean_row = mean_row + mean_z[peer]
    for b in range(1, batches):
        sum_group(b, None)

    def anomaly(wide):
        return (wide - jnp.mean(wide, axis=1, keepdims=True)).astype(BF16)

    def newton_weights(spread_low, mismatch, shift, b):
        cov = dot_nt(spread_low, spread_low) / (members - 1) + jnp.where(on_diag, var_ref[b:b + 1, :], 0.0)
        bound = jnp.max(jnp.sum(jnp.abs(cov), axis=1, keepdims=True), axis=0, keepdims=True)
        residual = ident - cov / bound
        approx = ident + residual
        for step in range(1, NEWTON):
            parts = split(residual)
            residual = dot3(parts, parts)
            approx = approx + dot3(split(approx), split(residual))
        innov = mismatch + shift
        return (dot3(split(approx), split(innov)) / bound).astype(BF16)

    state = ens[...].astype(F32)
    anom = anomaly(state)
    offsets = [
        as_column(obs_ref[b:b + 1, :] - mean_row[:, b * obs_count:(b + 1) * obs_count]) for b in range(batches)
    ]
    history = []
    for b in range(batches):
        loads[1 + batches + b].wait()
        prior = gathered(b)
        spread = prior.astype(F32)
        for earlier_low, earlier_weights in history:
            base = spread - jnp.mean(spread, axis=1, keepdims=True)
            hi, lo = split(base)
            cross = split((dot_nt(hi, earlier_low) + dot_nt(lo, earlier_low)) / (members - 1))
            spread = spread + jnp.dot(cross[0], earlier_weights, preferred_element_type=F32)
            spread = spread + jnp.dot(cross[1], earlier_weights, preferred_element_type=F32)
        mismatch = pert[b].astype(F32) - spread
        if history:
            spread = spread - jnp.mean(spread, axis=1, keepdims=True)
        spread_low = spread.astype(BF16)
        gain = (dot_nt(anom, spread_low) / (members - 1)).astype(BF16)
        weights = newton_weights(spread_low, mismatch, offsets[b], b)
        low = (state + jnp.dot(gain, weights, preferred_element_type=F32)).astype(BF16)
        history.append((spread_low, weights))
        if b + 1 < batches:
            state = low.astype(F32)
            anom = anomaly(state)
    out_ref[...] = low
    for copy in sends:
        copy.wait_send()


def on_device(ensemble, tiles, tile_live, observed, perturb, obs_var):
    region_count = lax.axis_size("region")
    group_count = lax.axis_size("group")
    batches, obs_count, members = perturb.shape
    chunk_rows = max(16, obs_count // region_count)
    chunk_cols = obs_count * members // (region_count * chunk_rows)
    vmem = pl.BlockSpec(memory_space=pltpu.VMEM)
    hbm = pl.BlockSpec(memory_space=pl.ANY)
    block = (chunk_rows, chunk_cols)
    dma = pltpu.SemaphoreType.DMA
    return pl.pallas_call(
        functools.partial(kernel, region_count, group_count),
        out_shape=pltpu.VMEM(ensemble.shape, ensemble.dtype),
        in_specs=[hbm, hbm, pl.BlockSpec(memory_space=pltpu.SMEM), vmem, hbm, vmem],
        out_specs=vmem,
        scratch_shapes=[
            pltpu.VMEM(ensemble.shape, BF16),
            pltpu.VMEM(tiles.shape, BF16),
            pltpu.VMEM(perturb.shape, BF16),
            pltpu.VMEM(perturb.shape, BF16),
            pltpu.VMEM((batches, region_count, *block), BF16),
            pltpu.VMEM((batches, *block), BF16),
            pltpu.VMEM((batches, group_count, *block), BF16),
            pltpu.VMEM(perturb.shape, BF16),
            pltpu.VMEM((1, batches * obs_count), F32),
            pltpu.VMEM((region_count, 1, batches * obs_count), F32),
            pltpu.VMEM((1, batches * obs_count), F32),
            pltpu.VMEM((group_count, 1, batches * obs_count), F32),
            pltpu.VMEM((batches, region_count // CORES, *block), BF16),
            pltpu.VMEM((batches, region_count // CORES, *block), BF16),
            dma((1 + 2 * batches,)),
            dma((batches * PIECES, region_count)),
            dma((batches * PIECES, region_count)),
            dma((batches * PIECES, group_count)),
            dma((batches * PIECES, group_count)),
            dma((batches * PIECES, region_count)),
            dma((batches * PIECES, region_count)),
            dma((region_count,)),
            dma((region_count,)),
            dma((group_count,)),
            dma((group_count,)),
            dma((batches, region_count // CORES)),
            dma((batches, region_count // CORES)),
        ],
        compiler_params=pltpu.CompilerParams(collective_id=0, has_side_effects=True),
    )(ensemble, tiles, tile_live, observed, perturb, obs_var)


def solution(mesh):
    return jax.shard_map(
        on_device,
        mesh=mesh,
        in_specs=(
            P(("region", "group"), None),
            P(None, None, ("region", "group")),
            P(),
            P(),
            P(),
            P(),
        ),
        out_specs=P(("region", "group"), None),
        check_vma=False,
    )
```

profile of v0, /device:TPU:0, one launch (start us, length us, event | category | flops | bytes accessed | tf_op | source)
XLA Modules:
  0.0 27.6 jit_solution(10085274268556726268)
XLA Ops:
  0.0 26.9 %shard_map.64 = bf16[256,512]{1,0:T(8,128)(2,1)S(1)} custom-call(bf16[256,512]{1,0:T(8,128)(2,1)} %ens_hbm.1, bf16[2,256,256]{2,1,0:T(8,128)(2,1)} %tiles_hbm.1, s32[2,8]{1,0:T(2,128)} %live_ref.1, f32[2,256]{1,0:T(2,128)} %obs_ref.1, bf16[2,256,512]{2,1,0:T(8,128)(2,1)} %pert_hbm.1, f32[2,256]{1,0:T(2,128)} %var_ref.1), custom_call_target="tpu_custom_call" | custom-call | tf_op jit(solution)/shard_map/pallas_call | solution.py:265
  26.9 0.7 %copy.8 = bf16[256,512]{1,0:T(8,128)(2,1)} copy(bf16[256,512]{1,0:T(8,128)(2,1)S(1)} %shard_map.64) | data formatting | bytes 524288
where the time goes:
time: 27.7 us; the launch traced here: 27.6 us
  Pallas kernels  26.9 us (97%)
  local copies, waits for them, and re-layouts  0.71 us (3%)
    pallas_call x1, Pallas kernels, on_device(): pl.pallas_call(functools.partial(kernel, region_count, group_count), out_...  26.9 us
    unnamed x1, local copies, waits for them, and re-layouts  0.71 us

commit v1 on v0

v1 whole, which is shorter than its diff:
```python
import functools

import jax
import jax.numpy as jnp
from jax import lax
from jax.experimental import pallas as pl
from jax.experimental.pallas import tpu as pltpu
from jax.sharding import PartitionSpec as P

NEWTON = 4
CORES = 2
PIECES = 2
F32 = jnp.float32
BF16 = jnp.bfloat16
MESH = pl.DeviceIdType.MESH


def split(x):
    hi = x.astype(BF16)
    return hi, (x - hi.astype(F32)).astype(BF16)


def dot3(a, b):
    left = jnp.concatenate([a[0], a[0], a[1]], axis=1)
    right = jnp.concatenate([b[0], b[1], b[0]], axis=0)
    return jnp.dot(left, right, preferred_element_type=F32)


def dot_nt(a, b):
    return lax.dot_general(a, b, (((1,), (1,)), ((), ())), preferred_element_type=F32)


def kernel(
    region_count, group_count,
    ens_hbm, tiles_hbm, live_hbm, obs_hbm, pert_hbm, var_hbm,
    out_ref,
    ens, tiles, live, obs, pert, var,
    partial, rs_buf, z_send, z_buf, spread_buf,
    mean_part, mean_rs, mean_zsend, mean_z,
    pair_buf, half_send, half_buf,
    load_sem, rs_sem, z_sem, ag_sem, mean_sem, pair_sem, half_sem,
):
    batches, obs_count, members = pert.shape
    region = lax.axis_index("region")
    group = lax.axis_index("group")
    chunk_rows, chunk_cols = z_send.shape[1:]
    across = members // chunk_cols

    barrier = pltpu.get_barrier_semaphore()
    region_peers = [lax.rem(region + k, region_count) for k in range(1, region_count)]
    group_peers = [lax.rem(group + k, group_count) for k in range(1, group_count)]
    for peer in region_peers:
        pl.semaphore_signal(barrier, inc=1, device_id=(peer, group), device_id_type=MESH)
    for peer in group_peers:
        pl.semaphore_signal(barrier, inc=1, device_id=(region, peer), device_id_type=MESH)

    sources = [(ens_hbm, ens)]
    sources += [(tiles_hbm.at[b], tiles.at[b]) for b in range(batches)]
    sources += [(live_hbm, live), (obs_hbm, obs), (var_hbm, var)]
    sources += [(pert_hbm.at[b], pert.at[b]) for b in range(batches)]
    loads = [pltpu.make_async_copy(src, dst, load_sem.at[i]) for i, (src, dst) in enumerate(sources)]
    early, late = loads[:4 + batches], loads[4 + batches:]
    for load in early:
        load.start()

    row_at = lax.broadcasted_iota(jnp.int32, (obs_count, obs_count), 0)
    col_at = lax.broadcasted_iota(jnp.int32, (obs_count, obs_count), 1)
    on_diag = row_at == col_at
    ident = jnp.where(on_diag, 1.0, 0.0).astype(F32)

    def as_row(column):
        return jnp.sum(jnp.where(on_diag, column, 0.0), axis=0, keepdims=True)

    def as_column(row):
        return jnp.sum(jnp.where(on_diag, row, 0.0), axis=1, keepdims=True)

    piece_cols = chunk_cols // PIECES

    def chunk(ref, index, piece=None):
        rows = pl.ds(pl.multiple_of(lax.div(index, across) * chunk_rows, chunk_rows), chunk_rows)
        start, width = (0, chunk_cols) if piece is None else (piece * piece_cols, piece_cols)
        if across > 1:
            start = pl.multiple_of(lax.rem(index, across) * chunk_cols + start, piece_cols)
        return ref.at[rows, pl.ds(start, width)]

    def cols(ref, piece):
        return ref if piece is None else ref.at[..., pl.ds(piece * piece_cols, piece_cols)]

    def slot_of(b, piece):
        return b * PIECES + (piece or 0)

    def pieces_of(b):
        return range(PIECES) if b == 0 else (None,)

    def remote(src, dst, sems, where):
        return pltpu.make_async_remote_copy(
            src_ref=src, dst_ref=dst, send_sem=sems.at[0], recv_sem=sems.at[1],
            device_id=where, device_id_type=MESH,
        )

    sends = []

    def phase(sems, whole):
        everything = remote(whole, whole, sems, (region, lax.rem(group + 1, group_count)))
        sends.append(everything)
        return everything

    def local_partial(b):
        loads[1 + b].wait()
        value = jnp.dot(tiles[b], ens[...], preferred_element_type=F32)
        value = value * live_of[b:b + 1]
        mean = jnp.mean(value, axis=1, keepdims=True)
        partial[b] = (value - mean).astype(BF16)
        return mean

    chips = region_count // CORES
    chip, core = lax.div(region, CORES), lax.rem(region, CORES)
    chip_peers = [lax.rem(chip + k, chips) for k in range(1, chips)]
    partner = chip * CORES + (CORES - 1 - core)

    phases = {}

    def scatter(b, piece):
        sems = rs_sem.at[slot_of(b, piece)]
        for k, peer in enumerate(region_peers):
            remote(chunk(partial.at[b], peer, piece), cols(rs_buf.at[k], piece), sems, (peer, group)).start()
        phases["rs", b, piece] = phase(sems, cols(rs_buf, piece))

    def scatter_pair(b):
        for k, there in enumerate(chip_peers + [chip]):
            sems = pair_sem.at[b - 1, k]
            remote(chunk(partial.at[b], there * CORES + CORES - 1 - core), pair_buf.at[b - 1, k], sems, (partner, group)).start()
            phases["pair", b, k] = phase(sems, pair_buf.at[b - 1, k])

    def pair_sum(b, k, there):
        phases["pair", b, k].wait_recv()
        return chunk(partial.at[b], there * CORES + core)[...].astype(F32) + pair_buf[b - 1, k].astype(F32)

    def scatter_chips(b):
        sems = half_sem.at[b - 1]
        for k, there in enumerate(chip_peers):
            half_send[b - 1, k] = pair_sum(b, k, there).astype(BF16)
            remote(half_send.at[b - 1, k], half_buf.at[b - 1, k], sems, (there * CORES + core, group)).start()
        phases["rs", b, None] = phase(sems, half_buf.at[b - 1])

    def sum_region(b, piece):
        if b == 0:
            total, buf = chunk(partial.at[b], region, piece)[...].astype(F32), cols(rs_buf, piece)
        else:
            total, buf = pair_sum(b, chips - 1, chip), half_buf.at[b - 1]
        phases["rs", b, piece].wait_recv()
        for k in range(buf.shape[0]):
            total = total + buf[k].astype(F32)
        mine = cols(z_send.at[b], piece)
        mine[...] = total.astype(BF16)
        sems = z_sem.at[slot_of(b, piece)]
        for k, peer in enumerate(group_peers):
            remote(mine, cols(z_buf.at[b, k], piece), sems, (region, peer)).start()
        phases["z", b, piece] = phase(sems, cols(z_buf.at[b], piece))

    def sum_group(b, piece):
        total = cols(z_send.at[b], piece)[...].astype(F32)
        phases["z", b, piece].wait_recv()
        for k in range(group_count - 1):
            total = total + cols(z_buf.at[b, k], piece)[...].astype(F32)
        mine = chunk(spread_buf.at[b], region, piece)
        mine[...] = total.astype(BF16)
        sems = ag_sem.at[slot_of(b, piece)]
        for k, peer in enumerate(region_peers):
            remote(mine, mine, sems, (peer, group)).start()
        phases["ag", b, piece] = phase(sems, cols(rs_buf, piece))

    def gathered(b):
        for piece in pieces_of(b):
            phases["ag", b, piece].wait_recv()
        return spread_buf[b]

    loads[1 + batches].wait()
    region_at = lax.broadcasted_iota(jnp.int32, live.shape, 1)
    live_of = jnp.sum(jnp.where(region_at == region, live[...].astype(F32), 0.0), axis=1, keepdims=True)
    loads[0].wait()
    means = [local_partial(0)]
    pl.semaphore_wait(barrier, region_count - 1 + group_count - 1)
    for piece in pieces_of(0):
        scatter(0, piece)
    for load in late:
        load.start()
    for b in range(1, batches):
        means.append(local_partial(b))
    for b in range(1, batches):
        scatter_pair(b)
    for b in range(batches):
        mean_part[:, b * obs_count:(b + 1) * obs_count] = as_row(means[b])
    for k, peer in enumerate(region_peers):
        remote(mean_part, mean_rs.at[k], mean_sem.at[0], (peer, group)).start()
    mean_region = phase(mean_sem.at[0], mean_rs)
    for b in range(1, batches):
        scatter_chips(b)
    for piece in pieces_of(0):
        sum_region(0, piece)
    total = mean_part[...]
    mean_region.wait_recv()
    for k in range(region_count - 1):
        total = total + mean_rs[k]
    mean_zsend[...] = total
    for k, peer in enumerate(group_peers):
        remote(mean_zsend, mean_z.at[k], mean_sem.at[1], (region, peer)).start()
    mean_group = phase(mean_sem.at[1], mean_z)
    for b in range(1, batches):
        sum_region(b, None)
    for piece in pieces_of(0):
        sum_group(0, piece)
    mean_row = mean_zsend[...]
    mean_group.wait_recv()
    for k in range(group_count - 1):
        mean_row = mean_row + mean_z[k]
    for b in range(1, batches):
        sum_group(b, None)
    for load in early[2 + batches:]:
        load.wait()

    def anomaly(wide):
        return (wide - jnp.mean(wide, axis=1, keepdims=True)).astype(BF16)

    def newton_weights(spread_low, mismatch, shift, b):
        cov = dot_nt(spread_low, spread_low) / (members - 1) + jnp.where(on_diag, var[b:b + 1, :], 0.0)
        bound = jnp.max(jnp.sum(jnp.abs(cov), axis=1, keepdims=True), axis=0, keepdims=True)
        residual = ident - cov / bound
        approx = ident + residual
        for step in range(1, NEWTON):
            parts = split(residual)
            residual = dot3(parts, parts)
            approx = approx + dot3(split(approx), split(residual))
        innov = mismatch + shift
        return (dot3(split(approx), split(innov)) / bound).astype(BF16)

    state = ens[...].astype(F32)
    anom = anomaly(state)
    offsets = [
        as_column(obs[b:b + 1, :] - mean_row[:, b * obs_count:(b + 1) * obs_count]) for b in range(batches)
    ]
    history = []
    for b in range(batches):
        late[b].wait()
        prior = gathered(b)
        spread = prior.astype(F32)
        for earlier_low, earlier_weights in history:
            base = spread - jnp.mean(spread, axis=1, keepdims=True)
            hi, lo = split(base)
            cross = split((dot_nt(hi, earlier_low) + dot_nt(lo, earlier_low)) / (members - 1))
            spread = spread + jnp.dot(cross[0], earlier_weights, preferred_element_type=F32)
            spread = spread + jnp.dot(cross[1], earlier_weights, preferred_element_type=F32)
        mismatch = pert[b].astype(F32) - spread
        if history:
            spread = spread - jnp.mean(spread, axis=1, keepdims=True)
        spread_low = spread.astype(BF16)
        gain = (dot_nt(anom, spread_low) / (members - 1)).astype(BF16)
        weights = newton_weights(spread_low, mismatch, offsets[b], b)
        low = (state + jnp.dot(gain, weights, preferred_element_type=F32)).astype(BF16)
        history.append((spread_low, weights))
        if b + 1 < batches:
            state = low.astype(F32)
            anom = anomaly(state)
    out_ref[...] = low
    for copy in sends:
        copy.wait_send()


def on_device(ensemble, tiles, tile_live, observed, perturb, obs_var):
    region_count = lax.axis_size("region")
    group_count = lax.axis_size("group")
    batches, obs_count, members = perturb.shape
    chunk_rows = max(16, obs_count // region_count)
    chunk_cols = obs_count * members // (region_count * chunk_rows)
    chips = region_count // CORES
    hbm = pl.BlockSpec(memory_space=pl.ANY)
    block = (chunk_rows, chunk_cols)
    dma = pltpu.SemaphoreType.DMA
    return pl.pallas_call(
        functools.partial(kernel, region_count, group_count),
        out_shape=pltpu.VMEM(ensemble.shape, ensemble.dtype),
        in_specs=[hbm] * 6,
        out_specs=pl.BlockSpec(memory_space=pltpu.VMEM),
        scratch_shapes=[
            pltpu.VMEM(ensemble.shape, BF16),
            pltpu.VMEM(tiles.shape, BF16),
            pltpu.VMEM(tile_live.shape, tile_live.dtype),
            pltpu.VMEM(observed.shape, F32),
            pltpu.VMEM(perturb.shape, BF16),
            pltpu.VMEM(obs_var.shape, F32),
            pltpu.VMEM(perturb.shape, BF16),
            pltpu.VMEM((region_count - 1, *block), BF16),
            pltpu.VMEM((batches, *block), BF16),
            pltpu.VMEM((batches, group_count - 1, *block), BF16),
            pltpu.VMEM(perturb.shape, BF16),
            pltpu.VMEM((1, batches * obs_count), F32),
            pltpu.VMEM((region_count - 1, 1, batches * obs_count), F32),
            pltpu.VMEM((1, batches * obs_count), F32),
            pltpu.VMEM((group_count - 1, 1, batches * obs_count), F32),
            pltpu.VMEM((batches - 1, chips, *block), BF16),
            pltpu.VMEM((batches - 1, chips - 1, *block), BF16),
            pltpu.VMEM((batches - 1, chips - 1, *block), BF16),
            dma((4 + 2 * batches,)),
            dma((PIECES, 2)),
            dma((batches * PIECES, 2)),
            dma((batches * PIECES, 2)),
            dma((2, 2)),
            dma((batches - 1, chips, 2)),
            dma((batches - 1, 2)),
        ],
        compiler_params=pltpu.CompilerParams(collective_id=0, has_side_effects=True),
    )(ensemble, tiles, tile_live, observed, perturb, obs_var)


def solution(mesh):
    return jax.shard_map(
        on_device,
        mesh=mesh,
        in_specs=(
            P(("region", "group"), None),
            P(None, None, ("region", "group")),
            P(),
            P(),
            P(),
            P(),
        ),
        out_specs=P(("region", "group"), None),
        check_vma=False,
    )
```

time: 27.7 us -> 25.4 us (0.917)
  Pallas kernels: 26.9 us -> 24.6 us
    pallas_call x1, Pallas kernels: 26.9 us -> 24.6 us  [on_device(): pl.pallas_call(functools.partial(kernel, region_count, group_count), out_...]
where the time goes in v1:
time: 25.4 us; the launch traced here: 25.3 us
  Pallas kernels  24.6 us (97%)
  local copies, waits for them, and re-layouts  0.71 us (3%)
    pallas_call x1, Pallas kernels, on_device(): pl.pallas_call(functools.partial(kernel, region_count, group_count), out_...  24.6 us
    unnamed x1, local copies, waits for them, and re-layouts  0.71 us

profile of v1, /device:TPU:0, one launch (start us, length us, event | category | flops | bytes accessed | tf_op | source)
XLA Modules:
  0.0 25.3 jit_solution(2500074251129282917)
XLA Ops:
  0.0 24.6 %shard_map.64 = bf16[256,512]{1,0:T(8,128)(2,1)S(1)} custom-call(bf16[256,512]{1,0:T(8,128)(2,1)} %ens_hbm.1, bf16[2,256,256]{2,1,0:T(8,128)(2,1)} %tiles_hbm.1, s32[2,8]{1,0:T(2,128)} %live_hbm.1, f32[2,256]{1,0:T(2,128)} %obs_hbm.1, bf16[2,256,512]{2,1,0:T(8,128)(2,1)} %pert_hbm.1, f32[2,256]{1,0:T(2,128)} %var_hbm.1), custom_call_target="tpu_custom_call" | custom-call | tf_op jit(solution)/shard_map/pallas_call | solution.py:279
  24.6 0.7 %copy.8 = bf16[256,512]{1,0:T(8,128)(2,1)} copy(bf16[256,512]{1,0:T(8,128)(2,1)S(1)} %shard_map.64) | data formatting | bytes 524288

commit v2 on v1

--- a/solution.py
+++ b/solution.py
@@ -15,15 +15,8 @@
 MESH = pl.DeviceIdType.MESH
 
 
-def split(x):
-    hi = x.astype(BF16)
-    return hi, (x - hi.astype(F32)).astype(BF16)
-
-
-def dot3(a, b):
-    left = jnp.concatenate([a[0], a[0], a[1]], axis=1)
-    right = jnp.concatenate([b[0], b[1], b[0]], axis=0)
-    return jnp.dot(left, right, preferred_element_type=F32)
+def dot(a, b):
+    return jnp.dot(a, b, preferred_element_type=F32)
 
 
 def dot_nt(a, b):
@@ -222,17 +215,24 @@
     def anomaly(wide):
         return (wide - jnp.mean(wide, axis=1, keepdims=True)).astype(BF16)
 
-    def newton_weights(spread_low, mismatch, shift, b):
+    def newton_weights(spread, spread_low, innov, b):
+        power = jnp.sum(jnp.sum(spread * spread, axis=0, keepdims=True), axis=1, keepdims=True) / (members - 1)
+        centre = (power + jnp.sum(var[b:b + 1, :], axis=1, keepdims=True)) / obs_count
         cov = dot_nt(spread_low, spread_low) / (members - 1) + jnp.where(on_diag, var[b:b + 1, :], 0.0)
-        bound = jnp.max(jnp.sum(jnp.abs(cov), axis=1, keepdims=True), axis=0, keepdims=True)
-        residual = ident - cov / bound
-        approx = ident + residual
+        rest = cov - jnp.where(on_diag, centre, 0.0)
+        low = rest.astype(BF16)
+        bound = jnp.max(jnp.sum(jnp.abs(cov), axis=0, keepdims=True), axis=1, keepdims=True)
+        inverse = 1.0 / bound
+        shift = 1.0 - centre * inverse
+        square = dot(low, low)
+        weights = (1.0 + shift) * innov - inverse * dot(low, innov.astype(BF16))
+        rest = (inverse * inverse) * square - (2.0 * shift * inverse) * rest
         for step in range(1, NEWTON):
-            parts = split(residual)
-            residual = dot3(parts, parts)
-            approx = approx + dot3(split(approx), split(residual))
-        innov = mismatch + shift
-        return (dot3(split(approx), split(innov)) / bound).astype(BF16)
+            shift = shift * shift
+            low = rest.astype(BF16)
+            weights, square = (1.0 + shift) * weights + dot(low, weights.astype(BF16)), dot(low, low)
+            rest = square + (2.0 * shift) * rest
+        return (weights * inverse).astype(BF16)
 
     state = ens[...].astype(F32)
     anom = anomaly(state)
@@ -244,19 +244,16 @@
         late[b].wait()
         prior = gathered(b)
         spread = prior.astype(F32)
+        mismatch = pert[b].astype(F32) - spread
         for earlier_low, earlier_weights in history:
-            base = spread - jnp.mean(spread, axis=1, keepdims=True)
-            hi, lo = split(base)
-            cross = split((dot_nt(hi, earlier_low) + dot_nt(lo, earlier_low)) / (members - 1))
-            spread = spread + jnp.dot(cross[0], earlier_weights, preferred_element_type=F32)
-            spread = spread + jnp.dot(cross[1], earlier_weights, preferred_element_type=F32)
-        mismatch = pert[b].astype(F32) - spread
-        if history:
-            spread = spread - jnp.mean(spread, axis=1, keepdims=True)
+            cross = (dot_nt(spread.astype(BF16), earlier_low) / (members - 1)).astype(BF16)
+            change = dot(cross, earlier_weights)
+            mismatch = mismatch - change
+            spread = spread + (change - jnp.mean(change, axis=1, keepdims=True))
         spread_low = spread.astype(BF16)
         gain = (dot_nt(anom, spread_low) / (members - 1)).astype(BF16)
-        weights = newton_weights(spread_low, mismatch, offsets[b], b)
-        low = (state + jnp.dot(gain, weights, preferred_element_type=F32)).astype(BF16)
+        weights = newton_weights(spread, spread_low, mismatch + offsets[b], b)
+        low = (state + dot(gain, weights)).astype(BF16)
         history.append((spread_low, weights))
         if b + 1 < batches:
             state = low.astype(F32)

time: 25.4 us -> 24.2 us (0.953)
  Pallas kernels: 24.6 us -> 23.4 us
    pallas_call x1, Pallas kernels: 24.6 us -> 23.4 us  [on_device(): pl.pallas_call(functools.partial(kernel, region_count, group_count), out_...]
where the time goes in v2:
time: 24.2 us; the launch traced here: 24.1 us
  Pallas kernels  23.4 us (97%)
  local copies, waits for them, and re-layouts  0.71 us (3%)
    pallas_call x1, Pallas kernels, on_device(): pl.pallas_call(functools.partial(kernel, region_count, group_count), out_...  23.4 us
    unnamed x1, local copies, waits for them, and re-layouts  0.71 us

profile of v2, /device:TPU:0, one launch (start us, length us, event | category | flops | bytes accessed | tf_op | source)
XLA Modules:
  0.0 24.1 jit_solution(9804011286579921413)
XLA Ops:
  0.0 23.4 %shard_map.64 = bf16[256,512]{1,0:T(8,128)(2,1)S(1)} custom-call(bf16[256,512]{1,0:T(8,128)(2,1)} %ens_hbm.1, bf16[2,256,256]{2,1,0:T(8,128)(2,1)} %tiles_hbm.1, s32[2,8]{1,0:T(2,128)} %live_hbm.1, f32[2,256]{1,0:T(2,128)} %obs_hbm.1, bf16[2,256,512]{2,1,0:T(8,128)(2,1)} %pert_hbm.1, f32[2,256]{1,0:T(2,128)} %var_hbm.1), custom_call_target="tpu_custom_call" | custom-call | tf_op jit(solution)/shard_map/pallas_call | solution.py:276
  23.4 0.7 %copy.8 = bf16[256,512]{1,0:T(8,128)(2,1)} copy(bf16[256,512]{1,0:T(8,128)(2,1)S(1)} %shard_map.64) | data formatting | bytes 524288

commit v3 on v2

v3 whole, which is shorter than its diff:
```python
import functools

import jax
import jax.numpy as jnp
from jax import lax
from jax.experimental import pallas as pl
from jax.experimental.pallas import tpu as pltpu
from jax.sharding import PartitionSpec as P

NEWTON = 4
CORES = 2
PLANES = 2
F32 = jnp.float32
BF16 = jnp.bfloat16
MESH = pl.DeviceIdType.MESH


def dot(a, b):
    return jnp.dot(a, b, preferred_element_type=F32)


def dot_nt(a, b):
    return lax.dot_general(a, b, (((1,), (1,)), ((), ())), preferred_element_type=F32)


def dot_tn(a, b):
    return lax.dot_general(a, b, (((0,), (0,)), ((), ())), preferred_element_type=F32)


def parts_of(batch, chunk_cols):
    half = chunk_cols // 2
    if batch == 0 and half % 128 == 0:
        return [(0, half, False, True), (half, half, True, False)]
    return [(0, chunk_cols, batch > 0, False)]


def kernel(
    region_count, group_count,
    ens_hbm, tiles_hbm, live_hbm, obs_hbm, pert_hbm, var_hbm,
    out_ref,
    ens, tiles, live, obs, pert, var,
    partial, direct, pair, half_send, half, z_send, z_buf, spread_buf,
    mean_part, mean_rs, mean_zsend, mean_z, all_sent,
    load_sem, send_sem, rs_sem, pair_sem, z_sem, ag_sem, hop_sem, mean_sem,
):
    batches, obs_count, members = pert.shape
    owners, chunk_rows, chunk_cols = partial.shape[1:]
    across = members // chunk_cols
    blocks = owners // across
    planes = owners // region_count
    sites = owners // CORES
    region = lax.axis_index("region")
    group = lax.axis_index("group")
    high, plane = lax.div(group, planes), lax.rem(group, planes)
    mine = plane * region_count + region
    site, core = lax.div(mine, CORES), lax.rem(mine, CORES)

    def others(me, count):
        peers = [k + (me <= k).astype(jnp.int32) for k in range(count - 1)]
        return [(peer, me - (me > peer).astype(jnp.int32)) for peer in peers]

    def device(owner):
        return lax.rem(owner, region_count), high * planes + lax.div(owner, region_count)

    near = others(mine, owners)
    near_sites = others(site, sites)
    far = [((region, there * planes + plane), slot) for there, slot in others(high, group_count // planes)]
    partner = device(site * CORES + CORES - 1 - core)

    barrier = pltpu.get_barrier_semaphore()
    for owner, _ in near:
        pl.semaphore_signal(barrier, inc=1, device_id=device(owner), device_id_type=MESH)
    for where, _ in far:
        pl.semaphore_signal(barrier, inc=1, device_id=where, device_id_type=MESH)

    sources = [(ens_hbm, ens)]
    sources += [(tiles_hbm.at[b], tiles.at[b]) for b in range(batches)]
    sources += [(live_hbm, live), (obs_hbm, obs), (var_hbm, var)]
    sources += [(pert_hbm.at[b], pert.at[b]) for b in range(batches)]
    loads = [pltpu.make_async_copy(src, dst, load_sem.at[i]) for i, (src, dst) in enumerate(sources)]
    early, late = loads[:4 + batches], loads[4 + batches:]
    for load in early:
        load.start()

    row_at = lax.broadcasted_iota(jnp.int32, (obs_count, obs_count), 0)
    col_at = lax.broadcasted_iota(jnp.int32, (obs_count, obs_count), 1)
    on_diag = row_at == col_at

    def as_row(column):
        return jnp.sum(jnp.where(on_diag, column, 0.0), axis=0, keepdims=True)

    def as_column(row):
        return jnp.sum(jnp.where(on_diag, row, 0.0), axis=1, keepdims=True)

    def remote(src, dst, recv_sem, where):
        return pltpu.make_async_remote_copy(
            src_ref=src, dst_ref=dst, send_sem=send_sem, recv_sem=recv_sem,
            device_id=where, device_id_type=MESH,
        )

    def arrived(ref, recv_sem):
        remote(ref, ref, recv_sem, partner).wait_recv()

    parts = [(b, *part) for b in range(batches) for part in parts_of(b, chunk_cols)]

    def cols(ref, part):
        return ref.at[..., pl.ds(parts[part][1], parts[part][2])]

    def of_batch(b):
        return [i for i, part in enumerate(parts) if part[0] == b]

    def local_partial(b):
        loads[1 + b].wait()
        value = dot(tiles[b], ens[...]) * live_of[b:b + 1]
        mean = jnp.mean(value, axis=1, keepdims=True)
        value = (value - mean).astype(BF16)
        for a in range(across):
            block = value[:, a * chunk_cols:(a + 1) * chunk_cols]
            partial[b, a * blocks:(a + 1) * blocks] = block.reshape(blocks, chunk_rows, chunk_cols)
        return mean

    def scatter_direct(i):
        b = parts[i][0]
        for owner, slot in near[::-1]:
            remote(cols(partial.at[b, owner], i), cols(direct.at[slot], i), rs_sem.at[i], device(owner)).start()

    def scatter_pair(i):
        b = parts[i][0]
        for k in range(sites):
            src = cols(partial.at[b, k * CORES + CORES - 1 - core], i)
            remote(src, cols(pair.at[b, k], i), pair_sem.at[i], partner).start()

    def scatter_sites(i):
        b = parts[i][0]
        arrived(cols(pair.at[b], i), pair_sem.at[i])
        for k, (there, slot) in list(enumerate(near_sites))[::-1]:
            total = cols(partial.at[b, there * CORES + core], i)[...].astype(F32) + cols(pair.at[b, there], i)[...].astype(F32)
            cols(half_send.at[b, k], i)[...] = total.astype(BF16)
            where = device(there * CORES + core)
            remote(cols(half_send.at[b, k], i), cols(half.at[b, slot], i), rs_sem.at[i], where).start()

    def sum_near(i):
        b = parts[i][0]
        total = cols(partial.at[b, mine], i)[...].astype(F32)
        if parts[i][3]:
            total = total + cols(pair.at[b, site], i)[...].astype(F32)
            arrivals = cols(half.at[b], i)
        else:
            arrivals = cols(direct, i)
        arrived(arrivals, rs_sem.at[i])
        for k in range(arrivals.shape[0]):
            total = total + arrivals[k].astype(F32)
        cols(z_send.at[b], i)[...] = total.astype(BF16)
        for where, slot in far:
            remote(cols(z_send.at[b], i), cols(z_buf.at[b, slot], i), z_sem.at[i], where).start()

    def sum_far(i):
        b = parts[i][0]
        total = cols(z_send.at[b], i)[...].astype(F32)
        arrived(cols(z_buf.at[b], i), z_sem.at[i])
        for k in range(len(far)):
            total = total + cols(z_buf.at[b, k], i)[...].astype(F32)
        ours = cols(spread_buf.at[b, mine], i)
        ours[...] = total.astype(BF16)
        if not parts[i][4]:
            for owner, _ in near:
                remote(ours, ours, ag_sem.at[i], device(owner)).start()
            return
        for there in range(sites // planes * (planes - 1)):
            owner = (there + jnp.where(there >= plane * (sites // planes), sites // planes, 0)) * CORES + core
            remote(ours, ours, hop_sem.at[0, i], device(owner)).start()
        for peer, _ in others(region, region_count):
            remote(ours, ours, ag_sem.at[i], device(plane * region_count + peer)).start()

    def pass_on(i):
        count = sites // planes * (planes - 1)
        arrived(cols(direct.at[pl.ds(0, count)], i), hop_sem.at[0, i])
        for there in range(count):
            owner = (there + jnp.where(there >= plane * (sites // planes), sites // planes, 0)) * CORES + core
            block = cols(spread_buf.at[parts[i][0], owner], i)
            remote(block, block, hop_sem.at[1, i], partner).start()

    def gathered(b):
        for i in of_batch(b):
            if parts[i][4]:
                arrived(cols(direct.at[pl.ds(0, sites // planes * (planes - 1))], i), hop_sem.at[1, i])
                arrived(cols(direct.at[pl.ds(0, region_count - 1)], i), ag_sem.at[i])
            else:
                arrived(cols(direct, i), ag_sem.at[i])
        blocks_of = [spread_buf[b, a * blocks:(a + 1) * blocks].reshape(obs_count, chunk_cols) for a in range(across)]
        return jnp.concatenate(blocks_of, axis=1) if across > 1 else blocks_of[0]

    loads[1 + batches].wait()
    region_at = lax.broadcasted_iota(jnp.int32, live.shape, 1)
    live_of = jnp.sum(jnp.where(region_at == region, live[...].astype(F32), 0.0), axis=1, keepdims=True)
    loads[0].wait()
    means = [local_partial(0)]
    pl.semaphore_wait(barrier, len(near) + len(far))
    for i in of_batch(0):
        if parts[i][3]:
            scatter_pair(i)
    for i in of_batch(0):
        if not parts[i][3]:
            scatter_direct(i)
    for load in late:
        load.start()
    for b in range(1, batches):
        means.append(local_partial(b))
        for i in of_batch(b):
            scatter_pair(i)
    for i in of_batch(0):
        if parts[i][3]:
            scatter_sites(i)
    for b in range(batches):
        mean_part[:, b * obs_count:(b + 1) * obs_count] = as_row(means[b])
    for owner, slot in near:
        remote(mean_part, mean_rs.at[slot], mean_sem.at[0], device(owner)).start()
    for b in range(1, batches):
        for i in of_batch(b):
            scatter_sites(i)
    for i in of_batch(0):
        sum_near(i)
    for b in range(1, batches):
        for i in of_batch(b):
            sum_near(i)
    for i in of_batch(0):
        sum_far(i)
    arrived(mean_rs, mean_sem.at[0])
    total = mean_part[...]
    for k in range(len(near)):
        total = total + mean_rs[k]
    mean_zsend[...] = total
    for where, slot in far:
        remote(mean_zsend, mean_z.at[slot], mean_sem.at[1], where).start()
    for b in range(1, batches):
        for i in of_batch(b):
            sum_far(i)
    for i, part in enumerate(parts):
        if part[4]:
            pass_on(i)
    arrived(mean_z, mean_sem.at[1])
    mean_row = mean_zsend[...]
    for k in range(len(far)):
        mean_row = mean_row + mean_z[k]
    for load in early[2 + batches:]:
        load.wait()

    def anomaly(wide):
        return (wide - jnp.mean(wide, axis=1, keepdims=True)).astype(BF16)

    def newton_weights(spread, spread_low, innov, b):
        power = jnp.sum(jnp.sum(spread * spread, axis=0, keepdims=True), axis=1, keepdims=True) / (members - 1)
        centre = (power + jnp.sum(var[b:b + 1, :], axis=1, keepdims=True)) / obs_count
        cov = dot_nt(spread_low, spread_low) / (members - 1) + jnp.where(on_diag, var[b:b + 1, :], 0.0)
        rest = cov - jnp.where(on_diag, centre, 0.0)
        low = rest.astype(BF16)
        bound = jnp.max(jnp.sum(jnp.abs(cov), axis=0, keepdims=True), axis=1, keepdims=True)
        inverse = 1.0 / bound
        shift = 1.0 - centre * inverse
        square = dot(low, low)
        weights = (1.0 + shift) * innov - inverse * dot(low, innov.astype(BF16))
        rest = (inverse * inverse) * square - (2.0 * shift * inverse) * rest
        for step in range(1, NEWTON):
            shift = shift * shift
            low = rest.astype(BF16)
            weights, square = (1.0 + shift) * weights + dot(low, weights.astype(BF16)), dot(low, low)
            rest = square + (2.0 * shift) * rest
        return weights * inverse

    def spread_out(column):
        return jnp.concatenate([column] * (members // column.shape[1]), axis=1)

    state = ens[...].astype(F32)
    anom = anomaly(state)
    targets = []
    for b in range(batches):
        late[b].wait()
        noise = pert[b].astype(F32)
        noise_mean = jnp.mean(noise, axis=1, keepdims=True)
        offset = as_column(obs[b:b + 1, :] - mean_row[:, b * obs_count:(b + 1) * obs_count])
        targets.append((noise - noise_mean, jnp.broadcast_to(noise_mean + offset, (obs_count, 128))))
    priors = [gathered(0)]
    crosses = []
    changes = []
    for b in range(batches):
        spread, middle = priors[b].astype(F32), targets[b][1]
        for k, (cross, earlier) in enumerate(zip(crosses, changes)):
            if k:
                cross = (dot_nt(spread.astype(BF16), history[k]) / (members - 1)).astype(BF16)
            change = dot(cross, earlier)
            spread = spread + change[:, :members]
            middle = middle - change[:, members:]
        spread_low = spread.astype(BF16)
        if b == 0:
            history = [spread_low]
        else:
            history.append(spread_low)
        gain = (dot_nt(anom, spread_low) / (members - 1)).astype(BF16)

        def between():
            priors.append(gathered(b + 1))
            crosses.append((dot_nt(priors[-1], history[0]) / (members - 1)).astype(BF16))

        innov = targets[b][0] - spread
        if b + 1 < batches:
            both = newton_weights(spread, spread_low, jnp.concatenate([innov, middle], axis=1), b)
            changes.append(both.astype(BF16))
            weights = both[:, :members] + spread_out(both[:, members:])
            between()
        else:
            weights = newton_weights(spread, spread_low, innov + spread_out(middle), b)
        low = (state + dot(gain, weights.astype(BF16))).astype(BF16)
        if b + 1 < batches:
            state = low.astype(F32)
            anom = anomaly(state)
    out_ref[...] = low
    pltpu.make_async_remote_copy(
        src_ref=all_sent, dst_ref=all_sent, send_sem=send_sem, recv_sem=send_sem,
        device_id=partner, device_id_type=MESH,
    ).wait_send()


def on_device(ensemble, tiles, tile_live, observed, perturb, obs_var):
    region_count = lax.axis_size("region")
    group_count = lax.axis_size("group")
    batches, obs_count, members = perturb.shape
    planes = PLANES if group_count % PLANES == 0 else 1
    owners = region_count * planes
    chunk_rows = max(16, obs_count // owners)
    chunk_cols = obs_count * members // (owners * chunk_rows)
    sites = owners // CORES
    far = group_count // planes - 1
    crossing = 2 * (sites // planes * (planes - 1))
    parts = [part for b in range(batches) for part in parts_of(b, chunk_cols)]
    rows = 2 * chunk_rows
    sent = sum(
        rows * width * ((sites + sites - 1 if pair else owners - 1) + far + (crossing + region_count - 1 if hop else owners - 1))
        for _, width, pair, hop in parts
    )
    sent += 4 * batches * obs_count * (owners - 1 + far)
    hbm = pl.BlockSpec(memory_space=pl.ANY)
    block = (chunk_rows, chunk_cols)
    dma = pltpu.SemaphoreType.DMA
    return pl.pallas_call(
        functools.partial(kernel, region_count, group_count),
        out_shape=pltpu.VMEM(ensemble.shape, ensemble.dtype),
        in_specs=[hbm] * 6,
        out_specs=pl.BlockSpec(memory_space=pltpu.VMEM),
        scratch_shapes=[
            pltpu.VMEM(ensemble.shape, BF16),
            pltpu.VMEM(tiles.shape, BF16),
            pltpu.VMEM(tile_live.shape, tile_live.dtype),
            pltpu.VMEM(observed.shape, F32),
            pltpu.VMEM(perturb.shape, BF16),
            pltpu.VMEM(obs_var.shape, F32),
            pltpu.VMEM((batches, owners, *block), BF16),
            pltpu.VMEM((owners - 1, *block), BF16),
            pltpu.VMEM((batches, sites, *block), BF16),
            pltpu.VMEM((batches, sites - 1, *block), BF16),
            pltpu.VMEM((batches, sites - 1, *block), BF16),
            pltpu.VMEM((batches, *block), BF16),
            pltpu.VMEM((batches, far, *block), BF16),
            pltpu.VMEM((batches, owners, *block), BF16),
            pltpu.VMEM((1, batches * obs_count), F32),
            pltpu.VMEM((owners - 1, 1, batches * obs_count), F32),
            pltpu.VMEM((1, batches * obs_count), F32),
            pltpu.VMEM((far, 1, batches * obs_count), F32),
            pltpu.VMEM((sent // 512, 128), F32),
            dma((4 + 2 * batches,)),
            dma(()),
            dma((len(parts),)),
            dma((len(parts),)),
            dma((len(parts),)),
            dma((len(parts),)),
            dma((2, 1)),
            dma((2,)),
        ],
        compiler_params=pltpu.CompilerParams(collective_id=0, has_side_effects=True),
    )(ensemble, tiles, tile_live, observed, perturb, obs_var)


def solution(mesh):
    return jax.shard_map(
        on_device,
        mesh=mesh,
        in_specs=(
            P(("region", "group"), None),
            P(None, None, ("region", "group")),
            P(),
            P(),
            P(),
            P(),
        ),
        out_specs=P(("region", "group"), None),
        check_vma=False,
    )
```

time: 24.2 us -> 22.4 us (0.926)
  Pallas kernels: 23.4 us -> 21.5 us
    pallas_call x1, Pallas kernels: 23.4 us -> 21.5 us  [on_device(): pl.pallas_call(functools.partial(kernel, region_count, group_count), out_...]
where the time goes in v3:
time: 22.4 us; the launch traced here: 22.2 us
  Pallas kernels  21.5 us (96%)
  local copies, waits for them, and re-layouts  0.71 us (3%)
    pallas_call x1, Pallas kernels, on_device(): pl.pallas_call(functools.partial(kernel, region_count, group_count), out_...  21.5 us
    unnamed x1, local copies, waits for them, and re-layouts  0.71 us

profile of v3, /device:TPU:0, one launch (start us, length us, event | category | flops | bytes accessed | tf_op | source)
XLA Modules:
  0.0 22.2 jit_solution(17496797576751815403)
XLA Ops:
  0.0 21.5 %shard_map.64 = bf16[256,512]{1,0:T(8,128)(2,1)S(1)} custom-call(bf16[256,512]{1,0:T(8,128)(2,1)} %ens_hbm.1, bf16[2,256,256]{2,1,0:T(8,128)(2,1)} %tiles_hbm.1, s32[2,8]{1,0:T(2,128)} %live_hbm.1, f32[2,256]{1,0:T(2,128)} %obs_hbm.1, bf16[2,256,512]{2,1,0:T(8,128)(2,1)} %pert_hbm.1, f32[2,256]{1,0:T(2,128)} %var_hbm.1), custom_call_target="tpu_custom_call" | custom-call | tf_op jit(solution)/shard_map/pallas_call | solution.py:344
  21.5 0.7 %copy.8 = bf16[256,512]{1,0:T(8,128)(2,1)} copy(bf16[256,512]{1,0:T(8,128)(2,1)S(1)} %shard_map.64) | data formatting | bytes 524288

commit v4 on v3

--- a/solution.py
+++ b/solution.py
@@ -62,6 +62,7 @@
     def device(owner):
         return lax.rem(owner, region_count), high * planes + lax.div(owner, region_count)
 
+    beyond = sites // planes * (planes - 1)
     near = others(mine, owners)
     near_sites = others(site, sites)
     far = [((region, there * planes + plane), slot) for there, slot in others(high, group_count // planes)]
@@ -75,8 +76,7 @@
 
     sources = [(ens_hbm, ens)]
     sources += [(tiles_hbm.at[b], tiles.at[b]) for b in range(batches)]
-    sources += [(live_hbm, live), (obs_hbm, obs), (var_hbm, var)]
-    sources += [(pert_hbm.at[b], pert.at[b]) for b in range(batches)]
+    sources += [(live_hbm, live), (obs_hbm, obs), (var_hbm, var), (pert_hbm, pert)]
     loads = [pltpu.make_async_copy(src, dst, load_sem.at[i]) for i, (src, dst) in enumerate(sources)]
     early, late = loads[:4 + batches], loads[4 + batches:]
     for load in early:
@@ -102,6 +102,9 @@
         remote(ref, ref, recv_sem, partner).wait_recv()
 
     parts = [(b, *part) for b in range(batches) for part in parts_of(b, chunk_cols)]
+
+    paired = [i for i, part in enumerate(parts) if part[3]]
+    hops = [i for i, part in enumerate(parts) if part[4]]
 
     def cols(ref, part):
         return ref.at[..., pl.ds(parts[part][1], parts[part][2])]
@@ -128,11 +131,11 @@
         b = parts[i][0]
         for k in range(sites):
             src = cols(partial.at[b, k * CORES + CORES - 1 - core], i)
-            remote(src, cols(pair.at[b, k], i), pair_sem.at[i], partner).start()
+            remote(src, cols(pair.at[b, k], i), pair_sem.at[paired.index(i)], partner).start()
 
     def scatter_sites(i):
         b = parts[i][0]
-        arrived(cols(pair.at[b], i), pair_sem.at[i])
+        arrived(cols(pair.at[b], i), pair_sem.at[paired.index(i)])
         for k, (there, slot) in list(enumerate(near_sites))[::-1]:
             total = cols(partial.at[b, there * CORES + core], i)[...].astype(F32) + cols(pair.at[b, there], i)[...].astype(F32)
             cols(half_send.at[b, k], i)[...] = total.astype(BF16)
@@ -168,27 +171,42 @@
             return
         for there in range(sites // planes * (planes - 1)):
             owner = (there + jnp.where(there >= plane * (sites // planes), sites // planes, 0)) * CORES + core
-            remote(ours, ours, hop_sem.at[0, i], device(owner)).start()
+            remote(ours, ours, hop_sem.at[0, hops.index(i)], device(owner)).start()
         for peer, _ in others(region, region_count):
             remote(ours, ours, ag_sem.at[i], device(plane * region_count + peer)).start()
 
     def pass_on(i):
         count = sites // planes * (planes - 1)
-        arrived(cols(direct.at[pl.ds(0, count)], i), hop_sem.at[0, i])
+        arrived(cols(direct.at[pl.ds(0, count)], i), hop_sem.at[0, hops.index(i)])
         for there in range(count):
             owner = (there + jnp.where(there >= plane * (sites // planes), sites // planes, 0)) * CORES + core
             block = cols(spread_buf.at[parts[i][0], owner], i)
-            remote(block, block, hop_sem.at[1, i], partner).start()
-
-    def gathered(b):
-        for i in of_batch(b):
-            if parts[i][4]:
-                arrived(cols(direct.at[pl.ds(0, sites // planes * (planes - 1))], i), hop_sem.at[1, i])
-                arrived(cols(direct.at[pl.ds(0, region_count - 1)], i), ag_sem.at[i])
-            else:
-                arrived(cols(direct, i), ag_sem.at[i])
-        blocks_of = [spread_buf[b, a * blocks:(a + 1) * blocks].reshape(obs_count, chunk_cols) for a in range(across)]
-        return jnp.concatenate(blocks_of, axis=1) if across > 1 else blocks_of[0]
+            remote(block, block, hop_sem.at[1, hops.index(i)], partner).start()
+
+    def wait_for(i):
+        if parts[i][4]:
+            arrived(cols(direct.at[pl.ds(0, beyond)], i), hop_sem.at[1, hops.index(i)])
+            arrived(cols(direct.at[pl.ds(0, region_count - 1)], i), ag_sem.at[i])
+        else:
+            arrived(cols(direct, i), ag_sem.at[i])
+
+    def gathered(b, use):
+        order = of_batch(b)[::-1]
+        if across > 1:
+            for i in order:
+                wait_for(i)
+            whole = [spread_buf[b, a * blocks:(a + 1) * blocks].reshape(obs_count, chunk_cols) for a in range(across)]
+            whole = jnp.concatenate(whole, axis=1)
+            return whole, use(whole, 0)
+        pieces, total = {}, None
+        for i in order:
+            wait_for(i)
+            start = parts[i][1]
+            pieces[start] = cols(spread_buf.at[b], i)[...].reshape(obs_count, parts[i][2])
+            made = use(pieces[start], start)
+            total = made if total is None else [x + y for x, y in zip(total, made)]
+        pieces = [pieces[start] for start in sorted(pieces)]
+        return (jnp.concatenate(pieces, axis=1) if len(pieces) > 1 else pieces[0]), total
 
     loads[1 + batches].wait()
     region_at = lax.broadcasted_iota(jnp.int32, live.shape, 1)
@@ -218,6 +236,18 @@
     for b in range(1, batches):
         for i in of_batch(b):
             scatter_sites(i)
+    def anomaly(wide):
+        return (wide - jnp.mean(wide, axis=1, keepdims=True)).astype(BF16)
+
+    for load in late:
+        load.wait()
+    state = ens[...].astype(F32)
+    anom = anomaly(state)
+    noise = []
+    for b in range(batches):
+        wide = pert[b].astype(F32)
+        middle = jnp.mean(wide, axis=1, keepdims=True)
+        noise.append((wide - middle, middle))
     for i in of_batch(0):
         sum_near(i)
     for b in range(1, batches):
@@ -245,13 +275,10 @@
     for load in early[2 + batches:]:
         load.wait()
 
-    def anomaly(wide):
-        return (wide - jnp.mean(wide, axis=1, keepdims=True)).astype(BF16)
-
-    def newton_weights(spread, spread_low, innov, b):
+    def newton_weights(spread, product, innov, b):
         power = jnp.sum(jnp.sum(spread * spread, axis=0, keepdims=True), axis=1, keepdims=True) / (members - 1)
         centre = (power + jnp.sum(var[b:b + 1, :], axis=1, keepdims=True)) / obs_count
-        cov = dot_nt(spread_low, spread_low) / (members - 1) + jnp.where(on_diag, var[b:b + 1, :], 0.0)
+        cov = product / (members - 1) + jnp.where(on_diag, var[b:b + 1, :], 0.0)
         rest = cov - jnp.where(on_diag, centre, 0.0)
         low = rest.astype(BF16)
         bound = jnp.max(jnp.sum(jnp.abs(cov), axis=0, keepdims=True), axis=1, keepdims=True)
@@ -270,49 +297,38 @@
     def spread_out(column):
         return jnp.concatenate([column] * (members // column.shape[1]), axis=1)
 
-    state = ens[...].astype(F32)
-    anom = anomaly(state)
     targets = []
     for b in range(batches):
-        late[b].wait()
-        noise = pert[b].astype(F32)
-        noise_mean = jnp.mean(noise, axis=1, keepdims=True)
         offset = as_column(obs[b:b + 1, :] - mean_row[:, b * obs_count:(b + 1) * obs_count])
-        targets.append((noise - noise_mean, jnp.broadcast_to(noise_mean + offset, (obs_count, 128))))
-    priors = [gathered(0)]
-    crosses = []
-    changes = []
+        targets.append((noise[b][0], jnp.broadcast_to(noise[b][1] + offset, (obs_count, 128))))
+    moves = []
     for b in range(batches):
-        spread, middle = priors[b].astype(F32), targets[b][1]
-        for k, (cross, earlier) in enumerate(zip(crosses, changes)):
-            if k:
-                cross = (dot_nt(spread.astype(BF16), history[k]) / (members - 1)).astype(BF16)
-            change = dot(cross, earlier)
+        def use(piece, start):
+            if b:
+                return []
+            return [dot_nt(piece, piece), dot_nt(anom[:, start:start + piece.shape[1]], piece)]
+
+        prior, made = gathered(b, use)
+        spread, middle = prior.astype(F32), targets[b][1]
+        for move in moves:
+            change = dot(spread.astype(BF16), move)
             spread = spread + change[:, :members]
             middle = middle - change[:, members:]
         spread_low = spread.astype(BF16)
-        if b == 0:
-            history = [spread_low]
-        else:
-            history.append(spread_low)
-        gain = (dot_nt(anom, spread_low) / (members - 1)).astype(BF16)
-
-        def between():
-            priors.append(gathered(b + 1))
-            crosses.append((dot_nt(priors[-1], history[0]) / (members - 1)).astype(BF16))
-
+        if b:
+            state = (state + dot(*update)).astype(BF16).astype(F32)
+            anom = anomaly(state)
+            made = [dot_nt(spread_low, spread_low), dot_nt(anom, spread_low)]
+        product, gain = made[0], (made[1] / (members - 1)).astype(BF16)
         innov = targets[b][0] - spread
         if b + 1 < batches:
-            both = newton_weights(spread, spread_low, jnp.concatenate([innov, middle], axis=1), b)
-            changes.append(both.astype(BF16))
+            both = newton_weights(spread, product, jnp.concatenate([innov, middle], axis=1), b)
+            moves.append((dot_tn(spread_low, both.astype(BF16)) / (members - 1)).astype(BF16))
             weights = both[:, :members] + spread_out(both[:, members:])
-            between()
+            update = gain, weights.astype(BF16)
         else:
-            weights = newton_weights(spread, spread_low, innov + spread_out(middle), b)
-        low = (state + dot(gain, weights.astype(BF16))).astype(BF16)
-        if b + 1 < batches:
-            state = low.astype(F32)
-            anom = anomaly(state)
+            weights = newton_weights(spread, product, innov + spread_out(middle), b)
+            low = (state + dot(gain, weights.astype(BF16))).astype(BF16)
     out_ref[...] = low
     pltpu.make_async_remote_copy(
         src_ref=all_sent, dst_ref=all_sent, send_sem=send_sem, recv_sem=send_sem,
@@ -366,13 +382,13 @@
             pltpu.VMEM((1, batches * obs_count), F32),
             pltpu.VMEM((far, 1, batches * obs_count), F32),
             pltpu.VMEM((sent // 512, 128), F32),
-            dma((4 + 2 * batches,)),
+            dma((5 + batches,)),
             dma(()),
             dma((len(parts),)),
+            dma((max(1, sum(part[2] for part in parts)),)),
             dma((len(parts),)),
             dma((len(parts),)),
-            dma((len(parts),)),
-            dma((2, 1)),
+            dma((2, max(1, sum(part[3] for part in parts)))),
             dma((2,)),
         ],
         compiler_params=pltpu.CompilerParams(collective_id=0, has_side_effects=True),

time: 22.4 us -> 22.4 us (level)
  no operation moved by 1% of the time
where the time goes in v4:
time: 22.4 us; the launch traced here: 22.2 us
  Pallas kernels  21.5 us (96%)
  local copies, waits for them, and re-layouts  0.71 us (3%)
    pallas_call x1, Pallas kernels, on_device(): pl.pallas_call(functools.partial(kernel, region_count, group_count), out_...  21.5 us
    unnamed x1, local copies, waits for them, and re-layouts  0.71 us

profile of v4, /device:TPU:0, one launch (start us, length us, event | category | flops | bytes accessed | tf_op | source)
XLA Modules:
  0.0 22.2 jit_solution(5300834382084529684)
XLA Ops:
  0.0 21.5 %shard_map.64 = bf16[256,512]{1,0:T(8,128)(2,1)S(1)} custom-call(bf16[256,512]{1,0:T(8,128)(2,1)} %ens_hbm.1, bf16[2,256,256]{2,1,0:T(8,128)(2,1)} %tiles_hbm.1, s32[2,8]{1,0:T(2,128)} %live_hbm.1, f32[2,256]{1,0:T(2,128)} %obs_hbm.1, bf16[2,256,512]{2,1,0:T(8,128)(2,1)} %pert_hbm.1, f32[2,256]{1,0:T(2,128)} %var_hbm.1), custom_call_target="tpu_custom_call" | custom-call | tf_op jit(solution)/shard_map/pallas_call | solution.py:360
  21.5 0.7 %copy.8 = bf16[256,512]{1,0:T(8,128)(2,1)} copy(bf16[256,512]{1,0:T(8,128)(2,1)S(1)} %shard_map.64) | data formatting | bytes 524288

commit v5 on v4

--- a/solution.py
+++ b/solution.py
@@ -62,7 +62,6 @@
     def device(owner):
         return lax.rem(owner, region_count), high * planes + lax.div(owner, region_count)
 
-    beyond = sites // planes * (planes - 1)
     near = others(mine, owners)
     near_sites = others(site, sites)
     far = [((region, there * planes + plane), slot) for there, slot in others(high, group_count // planes)]
@@ -169,24 +168,20 @@
             for owner, _ in near:
                 remote(ours, ours, ag_sem.at[i], device(owner)).start()
             return
-        for there in range(sites // planes * (planes - 1)):
-            owner = (there + jnp.where(there >= plane * (sites // planes), sites // planes, 0)) * CORES + core
-            remote(ours, ours, hop_sem.at[0, hops.index(i)], device(owner)).start()
-        for peer, _ in others(region, region_count):
-            remote(ours, ours, ag_sem.at[i], device(plane * region_count + peer)).start()
+        for there, _ in near_sites:
+            remote(ours, ours, hop_sem.at[0, hops.index(i)], device(there * CORES + core)).start()
+        remote(ours, ours, ag_sem.at[i], partner).start()
 
     def pass_on(i):
-        count = sites // planes * (planes - 1)
-        arrived(cols(direct.at[pl.ds(0, count)], i), hop_sem.at[0, hops.index(i)])
-        for there in range(count):
-            owner = (there + jnp.where(there >= plane * (sites // planes), sites // planes, 0)) * CORES + core
-            block = cols(spread_buf.at[parts[i][0], owner], i)
+        arrived(cols(direct.at[pl.ds(0, sites - 1)], i), hop_sem.at[0, hops.index(i)])
+        for there, _ in near_sites:
+            block = cols(spread_buf.at[parts[i][0], there * CORES + core], i)
             remote(block, block, hop_sem.at[1, hops.index(i)], partner).start()
 
     def wait_for(i):
         if parts[i][4]:
-            arrived(cols(direct.at[pl.ds(0, beyond)], i), hop_sem.at[1, hops.index(i)])
-            arrived(cols(direct.at[pl.ds(0, region_count - 1)], i), ag_sem.at[i])
+            arrived(cols(direct.at[pl.ds(0, sites - 1)], i), hop_sem.at[1, hops.index(i)])
+            arrived(cols(direct.at[0], i), ag_sem.at[i])
         else:
             arrived(cols(direct, i), ag_sem.at[i])
 
@@ -346,11 +341,10 @@
     chunk_cols = obs_count * members // (owners * chunk_rows)
     sites = owners // CORES
     far = group_count // planes - 1
-    crossing = 2 * (sites // planes * (planes - 1))
     parts = [part for b in range(batches) for part in parts_of(b, chunk_cols)]
     rows = 2 * chunk_rows
     sent = sum(
-        rows * width * ((sites + sites - 1 if pair else owners - 1) + far + (crossing + region_count - 1 if hop else owners - 1))
+        rows * width * ((sites + sites - 1 if pair else owners - 1) + far + (2 * (sites - 1) + 1 if hop else owners - 1))
         for _, width, pair, hop in parts
     )
     sent += 4 * batches * obs_count * (owners - 1 + far)

time: 22.4 us -> 22.3 us (level)
  no operation moved by 1% of the time
where the time goes in v5:
time: 22.3 us; the launch traced here: 22.1 us
  Pallas kernels  21.4 us (96%)
  local copies, waits for them, and re-layouts  0.71 us (3%)
    pallas_call x1, Pallas kernels, on_device(): pl.pallas_call(functools.partial(kernel, region_count, group_count), out_...  21.4 us
    unnamed x1, local copies, waits for them, and re-layouts  0.71 us

profile of v5, /device:TPU:0, one launch (start us, length us, event | category | flops | bytes accessed | tf_op | source)
XLA Modules:
  0.0 22.1 jit_solution(1039733098207798621)
XLA Ops:
  0.0 21.4 %shard_map.64 = bf16[256,512]{1,0:T(8,128)(2,1)S(1)} custom-call(bf16[256,512]{1,0:T(8,128)(2,1)} %ens_hbm.1, bf16[2,256,256]{2,1,0:T(8,128)(2,1)} %tiles_hbm.1, s32[2,8]{1,0:T(2,128)} %live_hbm.1, f32[2,256]{1,0:T(2,128)} %obs_hbm.1, bf16[2,256,512]{2,1,0:T(8,128)(2,1)} %pert_hbm.1, f32[2,256]{1,0:T(2,128)} %var_hbm.1), custom_call_target="tpu_custom_call" | custom-call | tf_op jit(solution)/shard_map/pallas_call | solution.py:354
  21.4 0.7 %copy.8 = bf16[256,512]{1,0:T(8,128)(2,1)} copy(bf16[256,512]{1,0:T(8,128)(2,1)S(1)} %shard_map.64) | data formatting | bytes 524288

commit v6 on v5

--- a/solution.py
+++ b/solution.py
@@ -210,11 +210,11 @@
     means = [local_partial(0)]
     pl.semaphore_wait(barrier, len(near) + len(far))
     for i in of_batch(0):
+        if not parts[i][3]:
+            scatter_direct(i)
+    for i in of_batch(0):
         if parts[i][3]:
             scatter_pair(i)
-    for i in of_batch(0):
-        if not parts[i][3]:
-            scatter_direct(i)
     for load in late:
         load.start()
     for b in range(1, batches):

time: 22.3 us -> 22.2 us (level)
  no operation moved by 1% of the time
where the time goes in v6:
time: 22.2 us; the launch traced here: 22 us
  Pallas kernels  21.3 us (96%)
  local copies, waits for them, and re-layouts  0.71 us (3%)
    pallas_call x1, Pallas kernels, on_device(): pl.pallas_call(functools.partial(kernel, region_count, group_count), out_...  21.3 us
    unnamed x1, local copies, waits for them, and re-layouts  0.71 us

profile of v6, /device:TPU:0, one launch (start us, length us, event | category | flops | bytes accessed | tf_op | source)
XLA Modules:
  0.0 22.0 jit_solution(9897958004914737184)
XLA Ops:
  0.0 21.3 %shard_map.64 = bf16[256,512]{1,0:T(8,128)(2,1)S(1)} custom-call(bf16[256,512]{1,0:T(8,128)(2,1)} %ens_hbm.1, bf16[2,256,256]{2,1,0:T(8,128)(2,1)} %tiles_hbm.1, s32[2,8]{1,0:T(2,128)} %live_hbm.1, f32[2,256]{1,0:T(2,128)} %obs_hbm.1, bf16[2,256,512]{2,1,0:T(8,128)(2,1)} %pert_hbm.1, f32[2,256]{1,0:T(2,128)} %var_hbm.1), custom_call_target="tpu_custom_call" | custom-call | tf_op jit(solution)/shard_map/pallas_call | solution.py:354
  21.3 0.7 %copy.8 = bf16[256,512]{1,0:T(8,128)(2,1)} copy(bf16[256,512]{1,0:T(8,128)(2,1)S(1)} %shard_map.64) | data formatting | bytes 524288
